TPU v7x, 32 devices: a whole 2x2x4 slice. The times are simulated.
32 devices in a mesh: seq: 8 (over z, x), head: 4 (over y, core).
Axes of the slice: x: 2, y: 2, z: 4, core: 2. Of those that a mesh axis runs over, the one named last changes fastest.
Arguments:
- queries: float32 [2048, 8192], P('seq', 'head'), may hold values from -8 to 8
- key_heads: float32 [2048, 1024], P('seq', 'head'), may hold values from -6 to 6
- value_heads: float32 [2048, 1024], P('seq', 'head'), may hold values from -6 to 6
- query_map: float32 [64, 128, 128], P('head'), may hold values from -0.5 to 0.5
- key_map: float32 [8, 128, 128], P('head'), may hold values from -0.5 to 0.5
Outputs:
- query_map_step: float32 [64, 128, 128], P('head')
- key_map_step: float32 [8, 128, 128], P('head')
All inputs are finite; a program needn't handle non-finite values.
Results may differ from a plain program's by a relative error of at most 0.00019.
Values sent between devices are 32-bit elements; how exact they have to be, the bound alone decides.
No kernel may reach another device: no remote copies, remote signals or barrier semaphores. Data moves between devices by JAX's collectives and lax.ppermute only.
A program may use at most 64 MiB of HBM per device.

v0:
```python
import jax
import jax.numpy as jnp
from jax import lax
from jax.sharding import PartitionSpec as P

HIGHEST = lax.Precision.HIGHEST
NEGATIVE = -1e30
EPSILON = 1e-06


def prefix(value, axis, join, neutral):
    count, mine = (lax.axis_size(axis), lax.axis_index(axis))
    pieces = jax.tree.map(lambda part: lax.all_gather(part, axis), value)
    total = jax.tree.map(
        lambda part, zero: jnp.full_like(part, 0) + jnp.asarray(zero, part.dtype), value, neutral
    )

    def hop(position, total):
        longer = join(total, jax.tree.map(lambda part: part[position], pieces))
        return jax.tree.map(lambda new, old: jnp.where(position < mine, new, old), longer, total)

    return lax.fori_loop(0, count - 1, hop, total)


def product(form, left, right):
    return jnp.einsum(form, left, right, precision=HIGHEST)


def add_pair(earlier, later):
    return (earlier[0] + later[0], earlier[1] + later[1])


def masked_total(gathered, own_index):
    number = gathered.shape[0]
    places = jnp.arange(number)
    chosen = places > own_index
    target_shape = (number,) + (1,) * (gathered.ndim - 1)
    return jnp.sum(jnp.where(chosen.reshape(target_shape), gathered, 0.0), axis=0)


def on_device(queries, key_heads, value_heads, query_map, key_map):
    tok_dev = queries.shape[0]
    kv_count = key_map.shape[0]
    query_count = query_map.shape[0]
    group_size = query_count // kv_count
    head_dim = key_map.shape[1]
    feat_dim = key_map.shape[2]
    seq_index = lax.axis_index("seq")
    my_start = seq_index * tok_dev
    my_last = my_start + tok_dev - 1
    query_four = queries.reshape(tok_dev, kv_count, group_size, head_dim).transpose(1, 2, 0, 3)
    key_three = key_heads.reshape(tok_dev, kv_count, head_dim)
    value_major = value_heads.reshape(tok_dev, kv_count, head_dim).transpose(1, 0, 2)
    map_four = query_map.reshape(kv_count, group_size, head_dim, feat_dim)
    query_pos = my_start + jnp.arange(tok_dev)
    inv_scale = head_dim ** (-0.5)

    def attend(running, block_keys, block_values, key_pos):
        run_top, run_total, run_accum = running
        allowed = query_pos[:, None] >= key_pos[None, :]
        scores = product("kgtd,ckd->kgtc", query_four, block_keys) * inv_scale
        masked = jnp.where(allowed, scores, NEGATIVE)
        new_top = jnp.maximum(run_top, jnp.max(masked, axis=-1))
        weights = jnp.where(allowed, jnp.exp(masked - new_top[..., None]), 0.0)
        rescale = jnp.exp(run_top - new_top)
        run_total = run_total * rescale + jnp.sum(weights, axis=-1)
        run_accum = run_accum * rescale[..., None] + product(
            "kgtc,ckd->kgtd", weights, block_values
        )
        return (new_top, run_total, run_accum)

    start_top = jnp.full((kv_count, group_size, tok_dev), NEGATIVE, jnp.float32)
    start_total = jnp.zeros((kv_count, group_size, tok_dev), jnp.float32)
    start_accum = jnp.zeros((kv_count, group_size, tok_dev, head_dim), jnp.float32)
    zero_state = jnp.zeros((kv_count, feat_dim, head_dim), jnp.float32)
    zero_norm = jnp.zeros((kv_count, feat_dim), jnp.float32)
    initial = (start_top, start_total, start_accum)
    shard_piece = (
        lax.all_gather(key_heads, "seq", axis=0, tiled=True),
        lax.all_gather(value_heads, "seq", axis=0, tiled=True),
    )
    rows_in = shard_piece[0].shape[0]
    step_rows = 1024
    blocks = rows_in // step_rows
    key_blocks = shard_piece[0].reshape(blocks, step_rows, kv_count, head_dim)
    value_blocks = shard_piece[1].reshape(blocks, step_rows, kv_count, head_dim)
    offsets = step_rows * jnp.arange(blocks)

    def block_step(running_state, block_data):
        block_keys, block_values, offset = block_data
        key_pos = offset + jnp.arange(step_rows)

        def compute(state_in):
            attended = attend(state_in[:3], block_keys, block_values, key_pos)
            return attended

        def keep(state_in):
            return state_in

        return (lax.cond(offset > my_last, keep, compute, running_state), None)

    result, _ = lax.scan(block_step, initial, (key_blocks, value_blocks, offsets))
    teacher = result[2] / result[1][..., None]
    query_act = product("kgtd,kgdf->kgtf", query_four, map_four)
    query_feat = jax.nn.softplus(query_act)
    key_act = product("tkd,kdf->ktf", key_three, key_map)
    key_feat = jax.nn.softplus(key_act)
    local_state = product("ktf,ktd->kfd", key_feat, value_major)
    local_norm = jnp.sum(key_feat, axis=1)
    state_prev, norm_prev = prefix(
        (local_state, local_norm), "seq", add_pair, (zero_state, zero_norm)
    )
    local_rows = jnp.arange(tok_dev)
    causal = local_rows[:, None] >= local_rows[None, :]
    kernel = jnp.where(causal, product("kgtf,ksf->kgts", query_feat, key_feat), 0.0)
    numerator = product("kgts,ksd->kgtd", kernel, value_major) + product(
        "kgtf,kfd->kgtd", query_feat, state_prev
    )
    denominator = jnp.sum(kernel, axis=-1) + product("kgtf,kf->kgt", query_feat, norm_prev)
    student = numerator / denominator[..., None]
    mismatch = student - teacher
    grad_num = mismatch / denominator[..., None]
    grad_den = -jnp.sum(mismatch * student, axis=-1) / denominator
    coupling = jnp.where(
        causal, product("kgtd,ksd->kgts", grad_num, value_major) + grad_den[..., None], 0.0
    )
    grad_query = (
        product("kgts,ksf->kgtf", coupling, key_feat)
        + product("kgtd,kfd->kgtf", grad_num, state_prev)
        + grad_den[..., None] * norm_prev[:, None, None, :]
    )
    adj_state = product("kgtf,kgtd->kfd", query_feat, grad_num)
    adj_norm = product("kgtf,kgt->kf", query_feat, grad_den)
    every_adj, every_adj_norm = (
        lax.all_gather(adj_state[None], "seq", axis=0, tiled=True),
        lax.all_gather(adj_norm[None], "seq", axis=0, tiled=True),
    )
    state_next = masked_total(every_adj, seq_index)
    norm_next = masked_total(every_adj_norm, seq_index)
    grad_key = (
        product("kgts,kgtf->ksf", coupling, query_feat)
        + product("ksd,kfd->ksf", value_major, state_next)
        + norm_next[:, None, :]
    )
    step_query = product("kgtd,kgtf->kgdf", query_four, grad_query * jax.nn.sigmoid(query_act))
    step_query = step_query.reshape(query_count, head_dim, feat_dim)
    step_key = product("tkd,ktf->kdf", key_three, grad_key * jax.nn.sigmoid(key_act))
    stacked = jnp.concatenate([step_query, step_key], axis=0)
    total_count = (query_count + kv_count) * lax.axis_size("head") * head_dim * feat_dim
    summed = lax.psum(stacked, "seq")
    square_sum = lax.psum(jnp.sum(summed * summed), "head")
    normalized = summed / jnp.sqrt(square_sum / total_count + EPSILON)
    return (normalized[:query_count], normalized[query_count:])


def solution(mesh):
    placed = (
        P("seq", "head"),
        P("seq", "head"),
        P("seq", "head"),
        P("head", None, None),
        P("head", None, None),
    )
    return jax.shard_map(
        on_device,
        mesh=mesh,
        in_specs=placed,
        out_specs=(P("head", None, None), P("head", None, None)),
        check_vma=False,
    )
```

profile of v0, /device:TPU:0, one launch (start us, length us, event | category | flops | bytes accessed | tf_op | source)
XLA Modules:
  0.0 465.7 jit_solution(18376853299022059545)
XLA Ops:
  7.2 1.5 fusion.66
  8.7 2.5 fusion.49
  11.3 0.7 all-gather.11.cloned.1.call-update
  12.0 0.7 all-gather.13.cloned.1.call-update
  12.8 0.6 iota_compare_fusion
  13.4 0.2 fusion.73
  13.6 0.8 copy.128
  14.4 0.5 iota_compare_fusion.1
  15.0 3.0 copy.48
  17.9 1.9 copy.57
  19.9 7.4 %fusion.48 = (u8[2,256,128]{2,1,0:T(8,128)(4,1)}, f32[2,8,256,128]{3,2,1,0:T(8,128)}) fusion(f32[2,8,256,128]{2,3,1,0:T(8,128)} %bitcast.155, f32[2,8,128,128]{3,2,1,0:T(8,128)S(1)} %bitcast.153), kind=kOutput, calls=%fused_computation.73 | convolution fusion | flops 807862272 | bytes 5308416 | tf_op jit(solution)/shard_map/kgtd,kgdf->kgtf/dot_general | solution.py:26
  27.3 22.5 %all-gather.4 = f32[8,2,128]{2,1,0:T(2,128)S(1)} all-gather(f32[1,2,128]{2,1,0:T(2,128)S(1)} %bitcast.163), channel_id=3, replica_groups=mesh['seq'=8,'head'=4] {'seq'}, dimensions={0}, use_global_device_ids=true | all-gather | bytes 9216 | tf_op jit(solution)/shard_map/all_gather | solution.py:13
  49.7 6.9 %select_reduce_fusion = (f32[2,8,256]{2,1,0:T(8,128)S(1)}, f32[2,8,256,256]{2,3,1,0:T(8,128)S(1)}) fusion(pred[256,256]{0,1:T(8,128)(4,1)} %iota_compare_fusion, f32[2,256,128]{2,1,0:T(8,128)S(1)} %copy-done.11, u8[256,128]{1,0:T(8,128)(4,1)} %copy-done.22, f32[2,8,256,128]{3,2,1,0:T(8,128)} %get-tuple-element.372, u8[2,256,128]{2,1,0:T(8,128)(4,1)} %get-tuple-element.371), kind=kOutput, calls=%fused_computation.30 | convolution fusion | flops 1618014208 | bytes 6733824 | tf_op jit(solution)/shard_map/kgtf,ksf->kgts/dot_general | solution.py:26
  56.7 3.9 fusion.20
  60.6 7.3 %while.32 = (s32[]{:T(128)}, f32[2,128,128]{2,1,0:T(8,128)S(1)}, f32[2,128]{1,0:T(2,128)S(1)}, s32[]{:T(128)}, f32[8,2,128,128]{3,2,1,0:T(8,128)}, /*index=5*/f32[8,2,128]{2,1,0:T(2,128)S(1)}, s32[]{:T(128)}, s32[]{:T(128)}) while((s32[]{:T(128)}, f32[2,128,128]{2,1,0:T(8,128)S(1)}, f32[2,128]{1,0:T(2,128)S(1)}, s32[]{:T(128)}, ...), condition=%wide.region_2.3_spmd.clone, body=%wide.region_1.2_spmd.clone.sunk | while | flops 99076 | bytes 396411 | solution.py:22
  60.9 0.9 add_select_fusion.20
  61.9 1.0 add_select_fusion.20
  62.9 1.0 add_select_fusion.20
  63.9 0.9 add_select_fusion.20
  64.9 0.9 add_select_fusion.20
  65.9 0.9 add_select_fusion.20
  66.9 0.9 add_select_fusion.20
  67.9 4.6 fusion.74
  72.6 0.6 bitcast_add_fusion
  73.2 31.2 %all-gather.11.cloned.1.call-done = f32[2048,256]{1,0:T(8,128)} async-done(((f32[256,256]{1,0:T(8,128)}), f32[2048,256]{1,0:T(8,128)}) %all-gather.11.cloned.1.call-update) | async-done | bytes 2097168 | tf_op jit(solution)/shard_map/all_gather | solution.py:79
  104.4 3.3 reshape.48
  107.7 3.0 copy.56
  110.7 43.5 %all-gather.13.cloned.1.call-done = f32[2048,256]{1,0:T(8,128)} async-done(((f32[256,256]{1,0:T(8,128)}), f32[2048,256]{1,0:T(8,128)}) %all-gather.13.cloned.1.call-update) | async-done | bytes 2097168 | tf_op jit(solution)/shard_map/all_gather | solution.py:80
  154.2 3.3 reshape.49
  157.5 3.1 copy.58
  160.6 1.5 max.21
  162.2 83.5 %while.31 = (s32[]{:T(128)}, f32[2,8,256]{2,1,0:T(8,128)S(1)}, f32[2,8,256]{2,1,0:T(8,128)S(1)}, f32[2,8,256,128]{3,2,1,0:T(8,128)}, s32[2]{0:T(128)S(1)}, /*ind...) while((s32[]{:T(128)}, f32[2,8,256]{2,1,0:T(8,128)S(1)}, ...), condition=%wide.region_9.10_spmd.clone, body=%wide.region_4.9_spmd.clone.sunk | while | flops 12936553472 | bytes 85218160 | solution.py:102
  183.3 0.6 dynamic_slice.53
  184.5 52.0 %conditional.3 = (f32[2,8,256]{2,1,0:T(8,128)S(1)}, f32[2,8,256]{2,1,0:T(8,128)S(1)}, f32[2,8,256,128]{3,2,1,0:T(8,128)}) conditional(s32[]{:T(128)} %convert_element_type.5, (s32[]{:T(128)}, s32[]{:T(128)}, s32[1024]{0:T(1024)S(1)}, f32[2,1024,2,128]{3,1,2,0:T(8,128)}, s32[]{:T(128)}, /*index=5*/f32[2,8,256,128]{3,2,1,0:T(8,128)S(1)}, ...), branch_computations={%region_5.7_spmd, %region_8.8_spmd} | conditional | flops 12936553472 | bytes 85180016 | solution.py:100
  184.6 0.6 broadcast_add_fusion
  185.2 0.2 broadcast_compare_fusion
  185.4 16.8 %fusion.2 = (f32[2,8,256]{2,1,0:T(8,128)S(1)}, f32[2,1024,8,256]{3,1,2,0:T(8,128)S(1)}) fusion(pred[256,1024]{0,1:T(8,128)(4,1)S(1)} %broadcast_compare_fusion, f32[2,8,256,128]{3,2,1,0:T(8,128)S(1)} %get-tuple-element.233, f32[2,1024,2,128]{3,1,2,0:T(8,128)} %get-tuple-element.231, s32[]{:T(128)} %get-tuple-element.232), kind=kOutput, calls=%fused_computation.3 | convolution fusion | flops 6455029760 | bytes 20201984 | tf_op jit(solution)/shard_map/while/body/eval_jaxpr/cond/branch_0_fun/kgtd,ckd->kgtc/dot_general | solution.py:26
  202.2 4.1 fusion.4
  206.4 28.9 %multiply_add_fusion = f32[2,8,256,128]{3,2,1,0:T(8,128)S(1)} fusion(f32[2,8,256,128]{3,2,1,0:T(8,128)S(1)} %copy-done.4, f32[2,1024,8,256]{3,1,2,0:T(8,128)S(1)} %get-tuple-element.366, f32[2,8,256]{2,1,0:T(8,128)S(1)} %max.16, pred[256,1024]{0,1:T(8,128)(4,1)S(1)} %broadcast_compare_fusion, f32[2,1024,2,128]{3,1,2,0:T(8,128)S(1)} %copy-done.15, ...), kind=kOutput, calls=%fused_computation.11 | convolution fusion | flops 6460276736 | bytes 22315012 | tf_op jit(solution)/shard_map/while/body/eval_jaxpr/cond/branch_0_fun/kgtc,ckd->kgtd/dot_general | solution.py:26
  235.3 1.3 copy-done.5
  236.6 0.6 dynamic_slice.53
  245.7 3.0 copy.59
  248.7 6.5 %multiply_reduce_fusion = (f32[2,8,256]{2,1,0:T(8,128)S(1)}, f32[2,8,256,128]{2,3,1,0:T(8,128)S(1)}) fusion(f32[2,8,256,128]{2,3,1,0:T(8,128)} %copy.59, f32[2,8,256]{2,1,0:T(8,128)S(1)} %get-tuple-element.260, f32[2,8,256]{2,1,0:T(8,128)S(1)} %copy-done.24, f32[2,8,256,128]{2,3,1,0:T(8,128)} %fusion.20, f32[2,128,128]{2,1,0:T(8,128)S(1)} %copy-done.7, ...), kind=kOutput, calls=%fused_computation.48 | convolution fusion | flops 813690880 | bytes 8634368 | tf_op jit(solution)/shard_map/kgtf,kfd->kgtd/dot_general | solution.py:26
  255.2 5.0 %fusion.50 = f32[2,8,256,256]{2,3,1,0:T(8,128)} fusion(f32[2,8,256,128]{2,3,1,0:T(8,128)S(1)} %get-tuple-element.368, f32[256,256]{1,0:T(8,128)S(1)} %copy-done.9), kind=kOutput, calls=%fused_computation.79 | convolution fusion | flops 1610612736 | bytes 6553600 | tf_op jit(solution)/shard_map/kgtd,ksd->kgts/dot_general | solution.py:26
  260.2 5.2 %convolution_bitcast_fusion.2 = f32[2,128,128]{2,1,0:T(8,128)} fusion(f32[2,8,256,128]{2,3,1,0:T(8,128)S(1)} %get-tuple-element.368, f32[2,8,256,128]{3,2,1,0:T(8,128)S(1)} %copy-done.16, u8[2,256,128]{2,1,0:T(8,128)(4,1)S(1)} %copy-done.26), kind=kOutput, calls=%fused_computation.66 | convolution fusion | flops 810024960 | bytes 4390912 | tf_op jit(solution)/shard_map/kgtf,kgtd->kfd/dot_general | solution.py:26
  265.6 9.0 %fusion.23 = f32[2,8,256,128]{3,2,1,0:T(8,128)S(1)} fusion(f32[2,8,256,256]{2,3,1,0:T(8,128)} %fusion.50, f32[2,8,256]{2,1,0:T(8,128)S(1)} %negate_divide_fusion, pred[256,256]{0,1:T(8,128)(4,1)S(1)} %copy-done.21, f32[2,256,128]{2,1,0:T(8,128)S(1)} %copy-done.12, u8[256,128]{1,0:T(8,128)(4,1)S(1)} %copy-done.23), kind=kOutput, calls=%fused_computation.34 | convolution fusion | flops 1613299712 | bytes 6668288 | tf_op jit(solution)/shard_map/kgts,ksf->kgtf/dot_general | solution.py:26
  274.6 3.4 fusion.63
  278.1 5.4 %fusion.24 = f32[2,8,128,128]{3,2,1,0:T(8,128)} fusion(f32[2,8,256,128]{2,3,1,0:T(8,128)S(1)} %bitcast.156, f32[2,8,256,128]{3,2,1,0:T(8,128)S(1)} %copy-done.17, f32[2,8,256,128]{3,2,1,0:T(8,128)S(1)} %fusion.23, f32[2,8,256,128]{3,2,1,0:T(8,128)S(1)} %fusion.63, f32[2,128]{1,0:T(2,128)S(1)} %copy-done.28, f32[2,8,256]{2,1,0:T(8,128)S(1)} %negate_divide_fusion), kind=kOutput, calls=%fused_computation.37 | convolution fusion | flops 808976384 | bytes 9454592 | tf_op jit(solution)/shard_map/kgtd,kgtf->kgdf/dot_general | solution.py:26
  283.5 1.7 copy.71
  285.2 0.2 copy-done.18
  285.4 2.3 fusion.67
  287.7 70.2 %all-gather.5 = f32[8,2,128]{2,1,0:T(2,128)S(1)} all-gather(f32[1,2,128]{2,1,0:T(2,128)S(1)} %bitcast.164), channel_id=5, replica_groups=mesh['seq'=8,'head'=4] {'seq'}, dimensions={0}, use_global_device_ids=true | all-gather | bytes 9216 | tf_op jit(solution)/shard_map/all_gather | solution.py:136
  358.1 6.9 %fusion.41 = f32[2,256,128]{2,1,0:T(8,128)S(1)} fusion(f32[2,8,256,256]{2,3,1,0:T(8,128)S(1)} %copy-done.3, f32[2,8,256]{2,1,0:T(8,128)S(1)} %negate_divide_fusion, pred[256,256]{0,1:T(8,128)(4,1)S(1)} %copy-done.21, f32[2,8,256,128]{3,2,1,0:T(8,128)} %get-tuple-element.372, u8[2,256,128]{2,1,0:T(8,128)(4,1)S(1)} %copy-done.26), kind=kOutput, calls=%fused_computation.60 | convolution fusion | flops 1617428480 | bytes 6701056 | tf_op jit(solution)/shard_map/kgts,kgtf->ksf/dot_general | solution.py:26
  365.0 1.4 select_reduce_fusion.1
  366.5 0.4 fusion.44
  366.9 0.6 convolution_bitcast_fusion.1
  367.5 0.1 copy.72
  367.6 1.1 pad_maximum_fusion
  368.8 77.7 %all-reduce.2.cloned.1.call-done = f32[18,128,128]{2,1,0:T(8,128)} async-done(((f32[18,128,128]{2,1,0:T(8,128)}), f32[18,128,128]{2,1,0:T(8,128)}) %all-reduce.2.cloned.1.call-update) | async-done | bytes 1179664 | tf_op jit(solution)/shard_map/psum | solution.py:150
  446.4 2.2 multiply_reduce_fusion.1
  448.6 6.4 %psum.15 = f32[]{:T(128)} all-reduce(f32[]{:T(128)} %multiply_reduce_fusion.1), channel_id=1, replica_groups=mesh['seq'=8,'head'=4] {'head'}, use_global_device_ids=true, to_apply=%region_15.16 | all-reduce | flops 1 | bytes 8 | tf_op jit(solution)/shard_map/psum | solution.py:151
  455.7 1.5 broadcast_divide_fusion.1
  457.2 1.1 slice.8
  458.3 0.7 slice.9
  (95 shorter events, 0.7 us)
Async XLA Ops:
  7.2 12.7 %copy-start = (f32[16,128,128]{2,1,0:T(8,128)S(1)}, f32[16,128,128]{2,1,0:T(8,128)}, u32[]{:S(2)}) copy-start(f32[16,128,128]{2,1,0:T(8,128)} %param.14) | copy-start | bytes 3145732
  7.2 6.4 %copy-start.8 = (f32[256,256]{1,0:T(8,128)S(1)}, f32[256,256]{1,0:T(8,128)}, u32[]{:S(2)}) copy-start(f32[256,256]{1,0:T(8,128)} %param.13) | copy-start | bytes 786436
  7.2 53.4 %all-gather.15.cloned.1.call-start = ((), (), s32[]{:S(2)}) async-start(), calls=%async_computation.3 | async-start | bytes 1179648 | tf_op jit(solution)/shard_map/all_gather | solution.py:13
  8.7 9.2 %copy-start.10 = (f32[2,256,128]{2,1,0:T(8,128)}, f32[2,256,128]{2,1,0:T(8,128)S(1)}, u32[]{:S(2)}) copy-start(f32[2,256,128]{2,1,0:T(8,128)S(1)} %get-tuple-element.370) | copy-start | bytes 786436
  8.7 9.2 %copy-start.22 = (u8[256,128]{1,0:T(8,128)(4,1)}, u8[256,128]{1,0:T(8,128)(4,1)S(1)}, u32[]{:S(2)}) copy-start(u8[256,128]{1,0:T(8,128)(4,1)S(1)} %get-tuple-element.369) | copy-start | bytes 98308
  11.2 93.2 %all-gather.11.cloned.1.call-start = ((), (), s32[]{:S(2)}) async-start(), calls=%async_computation | async-start | bytes 2359296 | tf_op jit(solution)/shard_map/all_gather | solution.py:79
  12.0 142.2 %all-gather.13.cloned.1.call-start = ((), (), s32[]{:S(2)}) async-start(), calls=%async_computation.1 | async-start | bytes 2359296 | tf_op jit(solution)/shard_map/all_gather | solution.py:80
  12.7 352.3 %all-gather.17.cloned.1.call-start = ((), (), s32[]{:S(2)}) async-start(), calls=%async_computation.4 | async-start | bytes 1179648 | tf_op jit(solution)/shard_map/all_gather | solution.py:135
  19.8 29.9 %copy-start.11 = (f32[2,256,128]{2,1,0:T(8,128)S(1)}, f32[2,256,128]{2,1,0:T(8,128)}, u32[]{:S(2)}) copy-start(f32[2,256,128]{2,1,0:T(8,128)} %copy-done.10) | copy-start | bytes 786436
  49.7 6.9 %copy-start.19 = (f32[256,256]{0,1:T(8,128)S(1)}, f32[256,256]{0,1:T(8,128)}, u32[]{:S(2)}) copy-start(f32[256,256]{0,1:T(8,128)} %copy.128) | copy-start | bytes 786436
  49.7 6.9 %copy-start.20 = (pred[256,256]{0,1:T(8,128)(4,1)S(1)}, pred[256,256]{0,1:T(8,128)(4,1)}, u32[]{:S(2)}) copy-start(pred[256,256]{0,1:T(8,128)(4,1)} %iota_compare_fusion) | copy-start | bytes 196612
  60.6 7.3 %copy-start.25 = (u8[2,256,128]{2,1,0:T(8,128)(4,1)S(1)}, u8[2,256,128]{2,1,0:T(8,128)(4,1)}, u32[]{:S(2)}) copy-start(u8[2,256,128]{2,1,0:T(8,128)(4,1)} %get-tuple-element.371) | copy-start | bytes 196612
  67.9 4.7 %copy-start.6 = (f32[2,128,128]{2,1,0:T(8,128)}, f32[2,128,128]{2,1,0:T(8,128)S(1)}, u32[]{:S(2)}) copy-start(f32[2,128,128]{2,1,0:T(8,128)S(1)} %get-tuple-element.257) | copy-start | bytes 393220
  67.9 4.7 %copy-start.27 = (f32[2,128]{1,0:T(2,128)}, f32[2,128]{1,0:T(2,128)S(1)}, u32[]{:S(2)}) copy-start(f32[2,128]{1,0:T(2,128)S(1)} %get-tuple-element.258) | copy-start | bytes 3076
  202.2 4.2 copy-start.4
  202.2 4.2 copy-start.15
  235.2 1.3 copy-start.5
  245.7 3.0 copy-start.7
  245.7 3.0 copy-start.24
  245.7 3.0 copy-start.26
  248.7 6.5 %copy-start.9 = (f32[256,256]{1,0:T(8,128)S(1)}, f32[256,256]{1,0:T(8,128)}, u32[]{:S(2)}) copy-start(f32[256,256]{1,0:T(8,128)} %param.13) | copy-start | bytes 786436
  255.2 5.0 %copy-start.16 = (f32[2,8,256,128]{3,2,1,0:T(8,128)S(1)}, f32[2,8,256,128]{3,2,1,0:T(8,128)}, u32[]{:S(2)}) copy-start(f32[2,8,256,128]{3,2,1,0:T(8,128)} %get-tuple-element.372) | copy-start | bytes 6291460
  260.2 5.3 %copy-start.12 = (f32[2,256,128]{2,1,0:T(8,128)S(1)}, f32[2,256,128]{2,1,0:T(8,128)}, u32[]{:S(2)}) copy-start(f32[2,256,128]{2,1,0:T(8,128)} %copy-done.10) | copy-start | bytes 786436
  260.2 5.3 %copy-start.21 = (pred[256,256]{0,1:T(8,128)(4,1)S(1)}, pred[256,256]{0,1:T(8,128)(4,1)}, u32[]{:S(2)}) copy-start(pred[256,256]{0,1:T(8,128)(4,1)} %iota_compare_fusion) | copy-start | bytes 196612
  260.2 5.3 %copy-start.23 = (u8[256,128]{1,0:T(8,128)(4,1)S(1)}, u8[256,128]{1,0:T(8,128)(4,1)}, u32[]{:S(2)}) copy-start(u8[256,128]{1,0:T(8,128)(4,1)} %copy-done.22) | copy-start | bytes 98308
  265.5 180.9 %all-reduce.2.cloned.1.call-start = ((), (), s32[]{:S(2)}) async-start(), calls=%async_computation.2 | async-start | bytes 2359296 | tf_op jit(solution)/shard_map/psum | solution.py:150
  274.6 3.5 copy-start.2
  274.6 3.5 copy-start.17
  274.6 3.5 copy-start.28
  283.5 1.9 copy-start.18
  285.4 72.6 %copy-start.29 = (pred[8]{0:T(512)(128)(4,1)S(1)}, pred[8]{0:T(512)(128)(4,1)}, u32[]{:S(2)}) copy-start(pred[8]{0:T(512)(128)(4,1)} %iota_compare_fusion.1) | copy-start | bytes 28
  285.4 72.7 %copy-start.3 = (f32[2,8,256,256]{2,3,1,0:T(8,128)S(1)}, f32[2,8,256,256]{2,3,1,0:T(8,128)}, u32[]{:S(2)}) copy-start(f32[2,8,256,256]{2,3,1,0:T(8,128)} %fusion.50) | copy-start | bytes 12582916
  358.1 6.9 %copy-start.30 = (pred[8]{0:T(512)(128)(4,1)S(1)}, pred[8]{0:T(512)(128)(4,1)}, u32[]{:S(2)}) copy-start(pred[8]{0:T(512)(128)(4,1)} %iota_compare_fusion.1) | copy-start | bytes 28
  358.1 8.3 %copy-start.13 = (f32[2,256,128]{2,1,0:T(8,128)S(1)}, f32[2,256,128]{2,1,0:T(8,128)}, u32[]{:S(2)}) copy-start(f32[2,256,128]{2,1,0:T(8,128)} %copy-done.10) | copy-start | bytes 786436
  365.0 1.9 copy-start.14
  455.7 3.3 copy-start.1
Sparse Core Ops, SparseCore 0:
  11.3 43.1 all-gather.14
  56.7 47.7 all-gather.10
  106.6 47.6 all-gather.12
  265.6 90.7 all-gather.16
  368.9 77.5 all-reduce.1
where the time goes:
time: 471 us; the launch traced here: 466 us
  waiting for transfers between devices  154 us (33%)
  matrix products  117 us (25%)
  blocking collectives  99.1 us (21%)
  loops' own time  30.9 us (7%)
  local copies, waits for them, and re-layouts  29.3 us (6%)
  other arithmetic  19.9 us (4%)
  between operations  15.2 us (3%)
    dot_general x18, matrix products, product(): return jnp.einsum(form, left, right, precision=HIGHEST)  117 us
    psum x1, waiting for transfers between devices, on_device(): summed = lax.psum(stacked, 'seq')  77.7 us
    all_gather x1, blocking collectives, on_device(): lax.all_gather(adj_norm[None], 'seq', axis=0, tiled=True)  70.2 us
    all_gather x1, waiting for transfers between devices, on_device(): lax.all_gather(value_heads, 'seq', axis=0, tiled=True)  43.5 us
    all_gather x1, waiting for transfers between devices, on_device(): lax.all_gather(key_heads, 'seq', axis=0, tiled=True)  31.2 us
    another operation x1, loops' own time, on_device(): lax.scan(block_step, initial, (key_blocks, value_blocks, offsets))  30.2 us
    all_gather x1, blocking collectives, prefix(): pieces = jax.tree.map(lambda part: lax.all_gather(part, axis), value)  22.5 us
    unnamed x60, local copies, waits for them, and re-layouts  11.4 us
  transfers between devices with their start and end apart: 5, of which 3 were waited for; matrix products, arithmetic and copies ran while one was open for 16% of the time, Pallas kernels for 0%

commit v1 on v0

--- a/solution.py
+++ b/solution.py
@@ -6,6 +6,14 @@
 HIGHEST = lax.Precision.HIGHEST
 NEGATIVE = -1e30
 EPSILON = 1e-06
+
+
+def gather_by_exchange(value, axis, dim):
+    peers = lax.axis_size(axis)
+    repeats = [peers if d == dim else 1 for d in range(value.ndim)]
+    return lax.all_to_all(
+        jnp.tile(value, repeats), axis, split_axis=dim, concat_axis=dim, tiled=True
+    )
 
 
 def prefix(value, axis, join, neutral):
@@ -77,7 +85,7 @@
     initial = (start_top, start_total, start_accum)
     shard_piece = (
         lax.all_gather(key_heads, "seq", axis=0, tiled=True),
-        lax.all_gather(value_heads, "seq", axis=0, tiled=True),
+        gather_by_exchange(value_heads, "seq", 0),
     )
     rows_in = shard_piece[0].shape[0]
     step_rows = 1024

time: 471 us -> 450 us (0.955)
  waiting for transfers between devices: 154 us -> 105 us
  blocking collectives: 99.1 us -> 117 us
  starting transfers between devices: 0.2 us -> 7.44 us
    all_gather x1 -> x0, waiting for transfers between devices: 43.5 us -> none  [on_device(): lax.all_gather(value_heads, 'seq', axis=0, tiled=True)]
    all_gather x1, blocking collectives: 22.5 us -> 40.8 us  [prefix(): pieces = jax.tree.map(lambda part: lax.all_gather(part, axis), value)]
    all_to_all x0 -> x1, starting transfers between devices: none -> 7.28 us  [gather_by_exchange(): lax.all_to_all(jnp.tile(value, repeats), axis, split_axis=dim, concat_axi...]
    unnamed x60 -> x58, local copies, waits for them, and re-layouts: 11.4 us -> 11.3 us
  transfers between devices with their start and end apart: 5 -> 5, of which waited for: 3 -> 2; matrix products, arithmetic and copies ran while one was open for 16% -> 17% of each run, Pallas kernels for 0% -> 0%
where the time goes in v1:
time: 450 us; the launch traced here: 444 us
  matrix products  117 us (26%)
  blocking collectives  117 us (26%)
  waiting for transfers between devices  105 us (23%)
  local copies, waits for them, and re-layouts  30.8 us (7%)
  loops' own time  30.8 us (7%)
  other arithmetic  19.9 us (4%)
  between operations  15.1 us (3%)
  starting transfers between devices  7.44 us (2%)
    dot_general x18, matrix products, product(): return jnp.einsum(form, left, right, precision=HIGHEST)  117 us
    psum x1, waiting for transfers between devices, on_device(): summed = lax.psum(stacked, 'seq')  77.7 us
    all_gather x1, blocking collectives, on_device(): lax.all_gather(adj_norm[None], 'seq', axis=0, tiled=True)  70.2 us
    all_gather x1, blocking collectives, prefix(): pieces = jax.tree.map(lambda part: lax.all_gather(part, axis), value)  40.8 us
    another operation x1, loops' own time, on_device(): lax.scan(block_step, initial, (key_blocks, value_blocks, offsets))  30.1 us
    all_gather x1, waiting for transfers between devices, on_device(): lax.all_gather(key_heads, 'seq', axis=0, tiled=True)  27 us
    unnamed x58, local copies, waits for them, and re-layouts  11.3 us
  transfers between devices with their start and end apart: 5, of which 2 were waited for; matrix products, arithmetic and copies ran while one was open for 17% of the time, Pallas kernels for 0%

profile of v1, /device:TPU:0, one launch (start us, length us, event | category | flops | bytes accessed | tf_op | source)
XLA Modules:
  0.0 444.3 jit_solution(266733649049353220)
XLA Ops:
  7.2 1.5 fusion.66
  8.7 2.5 fusion.49
  11.3 0.7 all-gather.10.cloned.1.call-update
  12.0 1.5 tile.2
  13.5 7.3 %all-to-all-start = ((f32[8,256,256]{2,1,0:T(8,128)}), f32[8,256,256]{2,1,0:T(8,128)}, u32[]{:S(2)}, u32[]{:S(2)}) async-start(f32[8,256,256]{2,1,0:T(8,128)} %tile.2), calls=%async_computation | async-start | bytes 4194304 | tf_op jit(solution)/shard_map/all_to_all | solution.py:14
  20.8 0.6 iota_compare_fusion
  21.5 0.2 fusion.73
  21.7 0.8 copy.128
  22.5 0.5 iota_compare_fusion.1
  23.1 3.0 copy.48
  26.0 1.9 copy.57
  27.9 7.4 %fusion.48 = (u8[2,256,128]{2,1,0:T(8,128)(4,1)}, f32[2,8,256,128]{3,2,1,0:T(8,128)}) fusion(f32[2,8,256,128]{2,3,1,0:T(8,128)} %bitcast.155, f32[2,8,128,128]{3,2,1,0:T(8,128)S(1)} %bitcast.153), kind=kOutput, calls=%fused_computation.73 | convolution fusion | flops 807862272 | bytes 5308416 | tf_op jit(solution)/shard_map/kgtd,kgdf->kgtf/dot_general | solution.py:34
  35.3 40.8 %all-gather.4 = f32[8,2,128]{2,1,0:T(2,128)S(1)} all-gather(f32[1,2,128]{2,1,0:T(2,128)S(1)} %bitcast.163), channel_id=3, replica_groups=mesh['seq'=8,'head'=4] {'seq'}, dimensions={0}, use_global_device_ids=true | all-gather | bytes 9216 | tf_op jit(solution)/shard_map/all_gather | solution.py:21
  76.1 6.9 %select_reduce_fusion = (f32[2,8,256]{2,1,0:T(8,128)S(1)}, f32[2,8,256,256]{2,3,1,0:T(8,128)S(1)}) fusion(pred[256,256]{0,1:T(8,128)(4,1)} %iota_compare_fusion, f32[2,256,128]{2,1,0:T(8,128)S(1)} %get-tuple-element.370, u8[256,128]{1,0:T(8,128)(4,1)} %copy-done.21, f32[2,8,256,128]{3,2,1,0:T(8,128)} %get-tuple-element.372, ...), kind=kOutput, calls=%fused_computation.30 | convolution fusion | flops 1618014208 | bytes 6733824 | tf_op jit(solution)/shard_map/kgtf,ksf->kgts/dot_general | solution.py:34
  83.1 4.0 fusion.20
  87.0 7.3 %while.32 = (s32[]{:T(128)}, f32[2,128,128]{2,1,0:T(8,128)S(1)}, f32[2,128]{1,0:T(2,128)S(1)}, s32[]{:T(128)}, f32[8,2,128,128]{3,2,1,0:T(8,128)}, /*index=5*/f32[8,2,128]{2,1,0:T(2,128)S(1)}, s32[]{:T(128)}, s32[]{:T(128)}) while((s32[]{:T(128)}, f32[2,128,128]{2,1,0:T(8,128)S(1)}, f32[2,128]{1,0:T(2,128)S(1)}, s32[]{:T(128)}, ...), condition=%wide.region_2.3_spmd.clone, body=%wide.region_1.2_spmd.clone.sunk | while | flops 99076 | bytes 396411 | solution.py:30
  87.3 0.9 add_select_fusion.20
  88.3 0.9 add_select_fusion.20
  89.3 0.9 add_select_fusion.20
  90.3 0.9 add_select_fusion.20
  91.3 1.0 add_select_fusion.20
  92.3 0.9 add_select_fusion.20
  93.3 0.9 add_select_fusion.20
  94.3 4.7 %fusion.74 = f32[2,1,8,256]{3,1,2,0:T(1,128)S(1)} fusion(f32[2,128,1,1]{1,2,3,0:T(1,128)S(1)} %bitcast.162, f32[2,8,256,128]{3,2,1,0:T(8,128)} %get-tuple-element.372, u8[2,256,128]{2,1,0:T(8,128)(4,1)S(1)} %copy-done.24), kind=kOutput, calls=%fused_computation.110 | convolution fusion | flops 11010048 | bytes 2180096 | tf_op jit(solution)/shard_map/kgtf,kf->kgt/dot_general | solution.py:34
  99.0 0.6 bitcast_add_fusion
  99.6 27.0 %all-gather.10.cloned.1.call-done = f32[2048,256]{1,0:T(8,128)} async-done(((f32[256,256]{1,0:T(8,128)}), f32[2048,256]{1,0:T(8,128)}) %all-gather.10.cloned.1.call-update) | async-done | bytes 2097168 | tf_op jit(solution)/shard_map/all_gather | solution.py:87
  126.6 3.2 reshape.56
  129.8 3.0 copy.56
  132.9 3.3 reshape.57
  136.2 3.1 copy.58
  139.3 1.6 max.21
  140.8 83.4 %while.31 = (s32[]{:T(128)}, f32[2,8,256]{2,1,0:T(8,128)S(1)}, f32[2,8,256]{2,1,0:T(8,128)S(1)}, f32[2,8,256,128]{3,2,1,0:T(8,128)}, s32[2]{0:T(128)S(1)}, /*ind...) while((s32[]{:T(128)}, f32[2,8,256]{2,1,0:T(8,128)S(1)}, ...), condition=%wide.region_9.10_spmd.clone, body=%wide.region_4.9_spmd.clone.sunk | while | flops 12936553472 | bytes 85218160 | solution.py:110
  162.0 0.6 dynamic_slice.53
  163.2 52.0 %conditional.3 = (f32[2,8,256]{2,1,0:T(8,128)S(1)}, f32[2,8,256]{2,1,0:T(8,128)S(1)}, f32[2,8,256,128]{3,2,1,0:T(8,128)}) conditional(s32[]{:T(128)} %convert_element_type.5, (s32[]{:T(128)}, s32[]{:T(128)}, s32[1024]{0:T(1024)S(1)}, f32[2,1024,2,128]{3,1,2,0:T(8,128)}, s32[]{:T(128)}, /*index=5*/f32[2,8,256,128]{3,2,1,0:T(8,128)S(1)}, ...), branch_computations={%region_5.7_spmd, %region_8.8_spmd} | conditional | flops 12936553472 | bytes 85180016 | solution.py:108
  163.2 0.6 broadcast_add_fusion
  163.8 0.2 broadcast_compare_fusion
  164.0 16.8 %fusion.2 = (f32[2,8,256]{2,1,0:T(8,128)S(1)}, f32[2,1024,8,256]{3,1,2,0:T(8,128)S(1)}) fusion(pred[256,1024]{0,1:T(8,128)(4,1)S(1)} %broadcast_compare_fusion, f32[2,8,256,128]{3,2,1,0:T(8,128)S(1)} %get-tuple-element.233, f32[2,1024,2,128]{3,1,2,0:T(8,128)} %get-tuple-element.231, s32[]{:T(128)} %get-tuple-element.232), kind=kOutput, calls=%fused_computation.3 | convolution fusion | flops 6455029760 | bytes 20201984 | tf_op jit(solution)/shard_map/while/body/eval_jaxpr/cond/branch_0_fun/kgtd,ckd->kgtc/dot_general | solution.py:34
  180.8 4.1 fusion.4
  184.9 28.9 %multiply_add_fusion = f32[2,8,256,128]{3,2,1,0:T(8,128)S(1)} fusion(f32[2,8,256,128]{3,2,1,0:T(8,128)S(1)} %copy-done.4, f32[2,1024,8,256]{3,1,2,0:T(8,128)S(1)} %get-tuple-element.366, f32[2,8,256]{2,1,0:T(8,128)S(1)} %max.16, pred[256,1024]{0,1:T(8,128)(4,1)S(1)} %broadcast_compare_fusion, f32[2,1024,2,128]{3,1,2,0:T(8,128)S(1)} %copy-done.14, ...), kind=kOutput, calls=%fused_computation.11 | convolution fusion | flops 6460276736 | bytes 22315012 | tf_op jit(solution)/shard_map/while/body/eval_jaxpr/cond/branch_0_fun/kgtc,ckd->kgtd/dot_general | solution.py:34
  213.8 1.3 copy-done.5
  215.2 0.6 dynamic_slice.53
  224.3 3.0 copy.59
  227.3 6.5 %multiply_reduce_fusion = (f32[2,8,256]{2,1,0:T(8,128)S(1)}, f32[2,8,256,128]{2,3,1,0:T(8,128)S(1)}) fusion(f32[2,8,256,128]{2,3,1,0:T(8,128)} %copy.59, f32[2,8,256]{2,1,0:T(8,128)S(1)} %get-tuple-element.260, f32[2,8,256]{2,1,0:T(8,128)S(1)} %copy-done.23, f32[2,8,256,128]{2,3,1,0:T(8,128)} %fusion.20, f32[2,128,128]{2,1,0:T(8,128)S(1)} %copy-done.7, ...), kind=kOutput, calls=%fused_computation.48 | convolution fusion | flops 813690880 | bytes 8634368 | tf_op jit(solution)/shard_map/kgtf,kfd->kgtd/dot_general | solution.py:34
  233.8 5.0 %fusion.50 = f32[2,8,256,256]{2,3,1,0:T(8,128)} fusion(f32[2,8,256,128]{2,3,1,0:T(8,128)S(1)} %get-tuple-element.368, f32[256,256]{1,0:T(8,128)S(1)} %copy-done.9), kind=kOutput, calls=%fused_computation.79 | convolution fusion | flops 1610612736 | bytes 6553600 | tf_op jit(solution)/shard_map/kgtd,ksd->kgts/dot_general | solution.py:34
  238.8 5.2 %convolution_bitcast_fusion.2 = f32[2,128,128]{2,1,0:T(8,128)} fusion(f32[2,8,256,128]{2,3,1,0:T(8,128)S(1)} %get-tuple-element.368, f32[2,8,256,128]{3,2,1,0:T(8,128)S(1)} %copy-done.15, u8[2,256,128]{2,1,0:T(8,128)(4,1)S(1)} %copy-done.25), kind=kOutput, calls=%fused_computation.66 | convolution fusion | flops 810024960 | bytes 4390912 | tf_op jit(solution)/shard_map/kgtf,kgtd->kfd/dot_general | solution.py:34
  244.1 9.0 %fusion.23 = f32[2,8,256,128]{3,2,1,0:T(8,128)S(1)} fusion(f32[2,8,256,256]{2,3,1,0:T(8,128)} %fusion.50, f32[2,8,256]{2,1,0:T(8,128)S(1)} %negate_divide_fusion, pred[256,256]{0,1:T(8,128)(4,1)S(1)} %copy-done.20, f32[2,256,128]{2,1,0:T(8,128)S(1)} %copy-done.11, u8[256,128]{1,0:T(8,128)(4,1)S(1)} %copy-done.22), kind=kOutput, calls=%fused_computation.34 | convolution fusion | flops 1613299712 | bytes 6668288 | tf_op jit(solution)/shard_map/kgts,ksf->kgtf/dot_general | solution.py:34
  253.1 3.4 fusion.63
  256.6 5.4 %fusion.24 = f32[2,8,128,128]{3,2,1,0:T(8,128)} fusion(f32[2,8,256,128]{2,3,1,0:T(8,128)S(1)} %bitcast.156, f32[2,8,256,128]{3,2,1,0:T(8,128)S(1)} %copy-done.16, f32[2,8,256,128]{3,2,1,0:T(8,128)S(1)} %fusion.23, f32[2,8,256,128]{3,2,1,0:T(8,128)S(1)} %fusion.63, f32[2,128]{1,0:T(2,128)S(1)} %copy-done.27, f32[2,8,256]{2,1,0:T(8,128)S(1)} %negate_divide_fusion), kind=kOutput, calls=%fused_computation.37 | convolution fusion | flops 808976384 | bytes 9454592 | tf_op jit(solution)/shard_map/kgtd,kgtf->kgdf/dot_general | solution.py:34
  262.1 1.7 copy.71
  263.8 0.2 copy-done.17
  264.0 2.3 fusion.67
  266.3 70.2 %all-gather.5 = f32[8,2,128]{2,1,0:T(2,128)S(1)} all-gather(f32[1,2,128]{2,1,0:T(2,128)S(1)} %bitcast.164), channel_id=5, replica_groups=mesh['seq'=8,'head'=4] {'seq'}, dimensions={0}, use_global_device_ids=true | all-gather | bytes 9216 | tf_op jit(solution)/shard_map/all_gather | solution.py:144
  336.6 6.9 %fusion.41 = f32[2,256,128]{2,1,0:T(8,128)S(1)} fusion(f32[2,8,256,256]{2,3,1,0:T(8,128)S(1)} %copy-done.3, f32[2,8,256]{2,1,0:T(8,128)S(1)} %negate_divide_fusion, pred[256,256]{0,1:T(8,128)(4,1)S(1)} %copy-done.20, f32[2,8,256,128]{3,2,1,0:T(8,128)} %get-tuple-element.372, u8[2,256,128]{2,1,0:T(8,128)(4,1)S(1)} %copy-done.25), kind=kOutput, calls=%fused_computation.60 | convolution fusion | flops 1617428480 | bytes 6701056 | tf_op jit(solution)/shard_map/kgts,kgtf->ksf/dot_general | solution.py:34
  343.6 1.4 select_reduce_fusion.1
  345.0 0.4 fusion.44
  345.4 0.6 convolution_bitcast_fusion.1
  346.1 0.1 copy.72
  346.2 1.1 pad_maximum_fusion
  347.3 77.7 %all-reduce.2.cloned.1.call-done = f32[18,128,128]{2,1,0:T(8,128)} async-done(((f32[18,128,128]{2,1,0:T(8,128)}), f32[18,128,128]{2,1,0:T(8,128)}) %all-reduce.2.cloned.1.call-update) | async-done | bytes 1179664 | tf_op jit(solution)/shard_map/psum | solution.py:158
  425.0 2.2 multiply_reduce_fusion.1
  427.1 6.4 %psum.15 = f32[]{:T(128)} all-reduce(f32[]{:T(128)} %multiply_reduce_fusion.1), channel_id=1, replica_groups=mesh['seq'=8,'head'=4] {'head'}, use_global_device_ids=true, to_apply=%region_15.16 | all-reduce | flops 1 | bytes 8 | tf_op jit(solution)/shard_map/psum | solution.py:159
  434.2 1.5 broadcast_divide_fusion.1
  435.7 1.1 slice.8
  436.8 0.7 slice.9
  (93 shorter events, 0.7 us)
Async XLA Ops:
  7.2 20.8 %copy-start = (f32[16,128,128]{2,1,0:T(8,128)S(1)}, f32[16,128,128]{2,1,0:T(8,128)}, u32[]{:S(2)}) copy-start(f32[16,128,128]{2,1,0:T(8,128)} %param.14) | copy-start | bytes 3145732
  7.2 4.8 %copy-start.8 = (f32[256,256]{1,0:T(8,128)S(1)}, f32[256,256]{1,0:T(8,128)}, u32[]{:S(2)}) copy-start(f32[256,256]{1,0:T(8,128)} %param.13) | copy-start | bytes 786436
  7.2 79.8 %all-gather.12.cloned.1.call-start = ((), (), s32[]{:S(2)}) async-start(), calls=%async_computation.3 | async-start | bytes 1179648 | tf_op jit(solution)/shard_map/all_gather | solution.py:21
  8.7 12.8 %copy-start.21 = (u8[256,128]{1,0:T(8,128)(4,1)}, u8[256,128]{1,0:T(8,128)(4,1)S(1)}, u32[]{:S(2)}) copy-start(u8[256,128]{1,0:T(8,128)(4,1)S(1)} %get-tuple-element.369) | copy-start | bytes 98308
  8.7 67.4 %copy-start.10 = (f32[2,256,128]{2,1,0:T(8,128)}, f32[2,256,128]{2,1,0:T(8,128)S(1)}, u32[]{:S(2)}) copy-start(f32[2,256,128]{2,1,0:T(8,128)S(1)} %get-tuple-element.370) | copy-start | bytes 786436
  11.2 115.4 %all-gather.10.cloned.1.call-start = ((), (), s32[]{:S(2)}) async-start(), calls=%async_computation.1 | async-start | bytes 2359296 | tf_op jit(solution)/shard_map/all_gather | solution.py:87
  13.5 119.4 %all-to-all-start = ((f32[8,256,256]{2,1,0:T(8,128)}), f32[8,256,256]{2,1,0:T(8,128)}, u32[]{:S(2)}, u32[]{:S(2)}) async-start(f32[8,256,256]{2,1,0:T(8,128)} %tile.2), calls=%async_computation | async-start | bytes 4194304 | tf_op jit(solution)/shard_map/all_to_all | solution.py:14
  20.8 322.8 %all-gather.14.cloned.1.call-start = ((), (), s32[]{:S(2)}) async-start(), calls=%async_computation.4 | async-start | bytes 1179648 | tf_op jit(solution)/shard_map/all_gather | solution.py:143
  76.1 6.9 %copy-start.18 = (f32[256,256]{0,1:T(8,128)S(1)}, f32[256,256]{0,1:T(8,128)}, u32[]{:S(2)}) copy-start(f32[256,256]{0,1:T(8,128)} %copy.128) | copy-start | bytes 786436
  76.1 6.9 %copy-start.19 = (pred[256,256]{0,1:T(8,128)(4,1)S(1)}, pred[256,256]{0,1:T(8,128)(4,1)}, u32[]{:S(2)}) copy-start(pred[256,256]{0,1:T(8,128)(4,1)} %iota_compare_fusion) | copy-start | bytes 196612
  87.0 7.3 %copy-start.24 = (u8[2,256,128]{2,1,0:T(8,128)(4,1)S(1)}, u8[2,256,128]{2,1,0:T(8,128)(4,1)}, u32[]{:S(2)}) copy-start(u8[2,256,128]{2,1,0:T(8,128)(4,1)} %get-tuple-element.371) | copy-start | bytes 196612
  94.3 4.7 %copy-start.6 = (f32[2,128,128]{2,1,0:T(8,128)}, f32[2,128,128]{2,1,0:T(8,128)S(1)}, u32[]{:S(2)}) copy-start(f32[2,128,128]{2,1,0:T(8,128)S(1)} %get-tuple-element.257) | copy-start | bytes 393220
  94.3 4.7 %copy-start.26 = (f32[2,128]{1,0:T(2,128)}, f32[2,128]{1,0:T(2,128)S(1)}, u32[]{:S(2)}) copy-start(f32[2,128]{1,0:T(2,128)S(1)} %get-tuple-element.258) | copy-start | bytes 3076
  180.8 4.2 copy-start.4
  180.8 4.2 copy-start.14
  213.8 1.3 copy-start.5
  224.2 3.0 copy-start.7
  224.2 3.0 copy-start.23
  224.2 3.0 copy-start.25
  227.2 6.5 %copy-start.9 = (f32[256,256]{1,0:T(8,128)S(1)}, f32[256,256]{1,0:T(8,128)}, u32[]{:S(2)}) copy-start(f32[256,256]{1,0:T(8,128)} %param.13) | copy-start | bytes 786436
  233.8 5.0 %copy-start.15 = (f32[2,8,256,128]{3,2,1,0:T(8,128)S(1)}, f32[2,8,256,128]{3,2,1,0:T(8,128)}, u32[]{:S(2)}) copy-start(f32[2,8,256,128]{3,2,1,0:T(8,128)} %get-tuple-element.372) | copy-start | bytes 6291460
  238.8 5.3 %copy-start.11 = (f32[2,256,128]{2,1,0:T(8,128)S(1)}, f32[2,256,128]{2,1,0:T(8,128)}, u32[]{:S(2)}) copy-start(f32[2,256,128]{2,1,0:T(8,128)} %copy-done.10) | copy-start | bytes 786436
  238.8 5.3 %copy-start.20 = (pred[256,256]{0,1:T(8,128)(4,1)S(1)}, pred[256,256]{0,1:T(8,128)(4,1)}, u32[]{:S(2)}) copy-start(pred[256,256]{0,1:T(8,128)(4,1)} %iota_compare_fusion) | copy-start | bytes 196612
  238.8 5.3 %copy-start.22 = (u8[256,128]{1,0:T(8,128)(4,1)S(1)}, u8[256,128]{1,0:T(8,128)(4,1)}, u32[]{:S(2)}) copy-start(u8[256,128]{1,0:T(8,128)(4,1)} %copy-done.21) | copy-start | bytes 98308
  244.1 180.9 %all-reduce.2.cloned.1.call-start = ((), (), s32[]{:S(2)}) async-start(), calls=%async_computation.2 | async-start | bytes 2359296 | tf_op jit(solution)/shard_map/psum | solution.py:158
  253.1 3.5 copy-start.2
  253.1 3.5 copy-start.16
  253.1 3.5 copy-start.27
  262.1 1.9 copy-start.17
  264.0 72.6 %copy-start.28 = (pred[8]{0:T(512)(128)(4,1)S(1)}, pred[8]{0:T(512)(128)(4,1)}, u32[]{:S(2)}) copy-start(pred[8]{0:T(512)(128)(4,1)} %iota_compare_fusion.1) | copy-start | bytes 28
  264.0 72.7 %copy-start.3 = (f32[2,8,256,256]{2,3,1,0:T(8,128)S(1)}, f32[2,8,256,256]{2,3,1,0:T(8,128)}, u32[]{:S(2)}) copy-start(f32[2,8,256,256]{2,3,1,0:T(8,128)} %fusion.50) | copy-start | bytes 12582916
  336.6 6.9 %copy-start.29 = (pred[8]{0:T(512)(128)(4,1)S(1)}, pred[8]{0:T(512)(128)(4,1)}, u32[]{:S(2)}) copy-start(pred[8]{0:T(512)(128)(4,1)} %iota_compare_fusion.1) | copy-start | bytes 28
  336.6 8.3 %copy-start.12 = (f32[2,256,128]{2,1,0:T(8,128)S(1)}, f32[2,256,128]{2,1,0:T(8,128)}, u32[]{:S(2)}) copy-start(f32[2,256,128]{2,1,0:T(8,128)} %copy-done.10) | copy-start | bytes 786436
  343.5 1.9 copy-start.13
  434.2 3.3 copy-start.1
Sparse Core Ops, SparseCore 0:
  11.3 64.7 all-gather.11
  78.3 48.3 all-gather.9
  244.2 90.7 all-gather.13
  347.4 77.5 all-reduce.1
